TPU v7x, 32 devices: a whole 2x2x4 slice. The times are simulated.
32 devices in a mesh: batch: 8 (over z, core), rows: 4 (over y, x).
Axes of the slice: x: 2, y: 2, z: 4, core: 2. Of those that a mesh axis runs over, the one named last changes fastest.
Arguments:
- x_clean: float32 [1024, 3, 16, 16], P('batch', None, 'rows'), may hold values from -1 to 1
- noise: float32 [1024, 3, 16, 16], P('batch', None, 'rows'), may hold values from -5 to 5
- timesteps: int32 [1024], P('batch'), may hold values from 0 to 999
- keep_mask: int32 [1024, 16, 16, 256], P('batch', 'rows'), may hold values 0 or 1
- adam_step: int32 [1], replicated, may hold values from 2 to 20
- inlet_weight: float32 [27, 256], replicated, may hold values from -1.25 to 1.25
- kernel_weight: float32 [2, 2304, 256], replicated, may hold values from -0.125 to 0.125
- attention_weight: float32 [4, 256, 256], replicated, may hold values from -0.375 to 0.375
- time_weight: float32 [640, 512], replicated, may hold values from -0.25 to 0.25
- shift_weight: float32 [512, 256], replicated, may hold values from -0.25 to 0.25
- outlet_weight: float32 [3, 2304], replicated, may hold values from -0.125 to 0.125
- small_params: float32 [19, 256], replicated, may hold values from 0.5 to 1.5
- state_inlet: float32 [2, 27, 256], replicated, as said below
- state_kernel: float32 [2, 2, 2304, 256], P(None, None, 'batch'), as said below
- state_attention: float32 [2, 4, 256, 256], P(None, None, 'batch'), as said below
- state_time: float32 [2, 640, 512], replicated, as said below
- state_shift: float32 [2, 512, 256], replicated, as said below
- state_outlet: float32 [2, 3, 2304], replicated, as said below
- state_small: float32 [2, 19, 256], replicated, as said below
- average_inlet: float32 [27, 256], replicated, may hold values from -1.25 to 1.25
- average_kernel: float32 [2, 2304, 256], P(None, 'batch'), may hold values from -0.125 to 0.125
- average_attention: float32 [4, 256, 256], P(None, 'batch'), may hold values from -0.375 to 0.375
- average_time: float32 [640, 512], replicated, may hold values from -0.25 to 0.25
- average_shift: float32 [512, 256], replicated, may hold values from -0.25 to 0.25
- average_outlet: float32 [3, 2304], replicated, may hold values from -0.125 to 0.125
- average_small: float32 [19, 256], replicated, may hold values from 0.5 to 1.5
Outputs:
- updated_inlet: float32 [2, 27, 256], replicated
- updated_kernel: float32 [2, 2, 2304, 256], replicated
- updated_attention: float32 [2, 4, 256, 256], replicated
- updated_time: float32 [2, 640, 512], replicated
- updated_shift: float32 [2, 512, 256], replicated
- updated_outlet: float32 [2, 3, 2304], replicated
- updated_small: float32 [2, 19, 256], replicated
- first_inlet: float32 [27, 256], replicated
- first_kernel: float32 [2, 2304, 256], P(None, 'batch')
- first_attention: float32 [4, 256, 256], P(None, 'batch')
- first_time: float32 [640, 512], replicated
- first_shift: float32 [512, 256], replicated
- first_outlet: float32 [3, 2304], replicated
- first_small: float32 [19, 256], replicated
- second_inlet: float32 [27, 256], replicated
- second_kernel: float32 [2, 2304, 256], P(None, 'batch')
- second_attention: float32 [4, 256, 256], P(None, 'batch')
- second_time: float32 [640, 512], replicated
- second_shift: float32 [512, 256], replicated
- second_outlet: float32 [3, 2304], replicated
- second_small: float32 [19, 256], replicated
- loss: float32 [], replicated
- gradient_norm: float32 [], replicated
Inputs may be any that keep to these rules, and one draw needn't show every extreme that they name: `state_inlet`: index 0 of each state holds first moments of both signs, index 1 positive second moments. `state_kernel`: as for state_inlet. `state_attention`: as for state_inlet. `state_time`: as for state_inlet. `state_shift`: as for state_inlet. `state_outlet`: as for state_inlet. `state_small`: as for state_inlet.
All inputs are finite; a program needn't handle non-finite values. No bound on the sum of `keep_mask` on one device may be relied on, other than what follows from the above.
Results may differ from a plain program's by a relative error of at most 0.0014.
The roundings to bfloat16 on the way count: a program that leaves them out, or rounds other values in their place, can miss the bound.
Values may be sent and summed in bfloat16 or wider, within the bound.
A program may use at most 640 MiB of HBM per device.

v0:
```python
import math

import jax
import jax.numpy as jnp
from jax import lax
from jax.sharding import PartitionSpec as P

G = 32


HIGH_PRECISION = lax.Precision.HIGHEST
CLIP = 0.05
GAMMA = 5.0
KEEP = 0.9
EPS_NORM = 1e-05
BETA_ONE = 0.9
BETA_TWO = 0.999
EPS_ADAM = 1e-08
DECAY = 0.01
EMA_TOP = 0.9999
RATES = (0.1, 0.01, 0.03, 0.05, 0.02, 0.01, 0.2)


def padded_2(block, sides, width):
    for axis, dim in sides:
        count = lax.axis_size(axis)
        forward = [(i, i + 1) for i in range(count - 1)]
        backward = [(target, source) for source, target in forward]
        low = lax.ppermute(
            lax.slice_in_dim(block, block.shape[dim] - width, None, axis=dim), axis, forward
        )
        high = lax.ppermute(lax.slice_in_dim(block, 0, width, axis=dim), axis, backward)
        block = jnp.concatenate([low, block, high], axis=dim)
    return block


def alpha_bars(timesteps):
    steps_all = jnp.arange(1000).astype(jnp.float32)
    beta_rates = 0.0001 + (0.02 - 0.0001) * steps_all / 999.0
    bar_table = jnp.exp(jnp.cumsum(jnp.log(1.0 - beta_rates)))
    one_hot = (timesteps[:, None] == jnp.arange(1000)[None, :]).astype(jnp.float32)
    return jnp.sum(one_hot * bar_table[None, :], axis=1)


def sinusoid(timesteps, width):
    half = width // 2
    rates = jnp.exp(-math.log(10000.0) * jnp.arange(half).astype(jnp.float32) / (half - 1))
    angles = timesteps.astype(jnp.float32)[:, None] * rates[None, :]
    return jnp.concatenate([jnp.sin(angles), jnp.cos(angles)], axis=1)


def widen(field):
    padded = padded_2(field, (("rows", 1),), 1)
    return jnp.pad(padded, ((0, 0), (0, 0), (1, 1), (0, 0)))


def widen_back(field):
    padded = padded_2(field, (("rows", 1),), 1)
    return jnp.pad(padded, ((0, 0), (0, 0), (1, 1), (0, 0)))


def gather_patches(padded):
    height = padded.shape[1] - 2
    breadth = padded.shape[2] - 2
    return jnp.concatenate(
        [
            padded[:, row_off : row_off + height, col_off : col_off + breadth, :]
            for row_off in range(3)
            for col_off in range(3)
        ],
        axis=3,
    )


def conv_apply(padded, weight):
    return jnp.einsum(
        "bhwk,kc->bhwc", gather_patches(padded), weight, preferred_element_type=jnp.float32
    )


def conv_weight_grad(padded, grad_out):
    return jnp.einsum(
        "bhwk,bhwc->kc", gather_patches(padded), grad_out, preferred_element_type=jnp.float32
    )


def conv_input_grad(grad_out, weight):
    inputs = weight.shape[0] // 9
    outputs = weight.shape[1]
    flipped = jnp.transpose(weight.reshape(9, inputs, outputs)[::-1], (0, 2, 1)).reshape(
        9 * outputs, inputs
    )
    return conv_apply(widen_back(grad_out), flipped)


def grouped_view(field):
    return field.reshape(field.shape[0], -1, G, field.shape[3] // G)


def norm_stats(field):
    grouped = grouped_view(field)
    total = jnp.sum(grouped, axis=(1, 3))
    square = jnp.sum(grouped * grouped, axis=(1, 3))
    count = grouped.shape[1] * grouped.shape[3]
    total, square = (
        lax.psum(total.astype(jnp.bfloat16), "rows").astype(jnp.float32),
        lax.psum(square.astype(jnp.bfloat16), "rows").astype(jnp.float32),
    )
    count = count * lax.axis_size("rows")
    mean = total / count
    return (mean, lax.rsqrt(square / count - mean * mean + EPS_NORM))


def standard(field, stats):
    grouped = grouped_view(field)
    return ((grouped - stats[0][:, None, :, None]) * stats[1][:, None, :, None]).reshape(
        field.shape
    )


def norm_back(grad_out, field, stats, gain):
    normed = standard(field, stats)
    gain_grad = jnp.sum(grad_out * normed, axis=(0, 1, 2))
    shift_grad = jnp.sum(grad_out, axis=(0, 1, 2))
    scaled = grouped_view(grad_out * gain)
    grouped = grouped_view(normed)
    first_sum = jnp.sum(scaled, axis=(1, 3))
    second_sum = jnp.sum(scaled * grouped, axis=(1, 3))
    count = grouped.shape[1] * grouped.shape[3]
    first_sum, second_sum = (
        lax.psum(first_sum.astype(jnp.bfloat16), "rows").astype(jnp.float32),
        lax.psum(second_sum.astype(jnp.bfloat16), "rows").astype(jnp.float32),
    )
    count = count * lax.axis_size("rows")
    input_grad = (
        scaled
        - first_sum[:, None, :, None] / count
        - grouped * second_sum[:, None, :, None] / count
    ) * stats[1][:, None, :, None]
    return (input_grad.reshape(field.shape), gain_grad, shift_grad)


def swish_grad(pre):
    logistic = jax.nn.sigmoid(pre)
    return logistic * (1.0 + pre * (1.0 - logistic))


def attend(query_rows, key_rows, value_rows):
    attention_scores = jnp.einsum(
        "zji,zxi->zjx", query_rows, key_rows, preferred_element_type=jnp.float32
    ) * query_rows.shape[2] ** (-0.5)
    top = jnp.max(attention_scores, axis=-1, keepdims=True)
    expo = jnp.exp(attention_scores - top)
    total = jnp.sum(expo, axis=-1, keepdims=True)
    weight_tensors = (expo / total).astype(jnp.bfloat16)
    attended_tokens = jnp.einsum(
        "pvg,pgj->pvj", weight_tensors, value_rows, preferred_element_type=jnp.float32
    )
    return (attended_tokens.astype(jnp.bfloat16), top + jnp.log(total))


def attend_back(query_rows, key_rows, value_rows, logsum, gradient_mixed_tokens):
    scale_factor = query_rows.shape[2] ** (-0.5)
    attention_scores = (
        jnp.einsum("zji,zxi->zjx", query_rows, key_rows, preferred_element_type=jnp.float32)
        * scale_factor
    )
    softmax_probs = jnp.exp(attention_scores - logsum)
    gradient_softmax_probs = jnp.einsum(
        "zji,zxi->zjx", gradient_mixed_tokens, value_rows, preferred_element_type=jnp.float32
    )
    value_grad = jnp.einsum(
        "jio,jiz->joz",
        softmax_probs.astype(jnp.bfloat16),
        gradient_mixed_tokens,
        preferred_element_type=jnp.float32,
    )
    scores_gradient = (
        softmax_probs
        * (
            gradient_softmax_probs
            - jnp.sum(softmax_probs * gradient_softmax_probs, axis=-1, keepdims=True)
        )
    ).astype(jnp.bfloat16)
    query_grad = (
        jnp.einsum("pvg,pgj->pvj", scores_gradient, key_rows, preferred_element_type=jnp.float32)
        * scale_factor
    )
    key_grad = (
        jnp.einsum("jio,jiz->joz", scores_gradient, query_rows, preferred_element_type=jnp.float32)
        * scale_factor
    )
    return (query_grad, key_grad, value_grad)


def adam(weight, state, average, grad, rate, count):
    first_new = BETA_ONE * state[0] + (1.0 - BETA_ONE) * grad
    second_new = BETA_TWO * state[1] + (1.0 - BETA_TWO) * grad * grad
    first_hat = first_new / (1.0 - BETA_ONE**count)
    second_hat = second_new / (1.0 - BETA_TWO**count)
    weight_new = weight - rate * (first_hat / (jnp.sqrt(second_hat) + EPS_ADAM) + DECAY * weight)
    keep = jnp.minimum(EMA_TOP, (1.0 + count) / (10.0 + count))
    average_new = keep * average + (1.0 - keep) * weight_new
    return (jnp.stack([weight_new, average_new]), first_new, second_new)


def local(
    x_clean,
    noise,
    timesteps,
    keep_mask,
    adam_step,
    inlet_weight,
    kernel_weight,
    attention_weight,
    time_weight,
    shift_weight,
    outlet_weight,
    small_params,
    state_inlet,
    state_kernel,
    state_attention,
    state_time,
    state_shift,
    state_outlet,
    state_small,
    average_inlet,
    average_kernel,
    average_attention,
    average_time,
    average_shift,
    average_outlet,
    average_small,
):
    chans = kernel_weight.shape[2]
    width_sin = time_weight.shape[0] - time_weight.shape[1]
    bars = alpha_bars(timesteps)
    level = bars[:, None, None, None]
    clean = jnp.transpose(x_clean, (0, 2, 3, 1))
    target = jnp.transpose(noise, (0, 2, 3, 1))
    noisy = (jnp.sqrt(level) * clean + jnp.sqrt(1.0 - level) * target).astype(jnp.bfloat16)
    dropped = keep_mask.astype(jnp.float32) / KEEP
    images, height, breadth = (noisy.shape[0], noisy.shape[1], noisy.shape[2])
    inlet = inlet_weight.astype(jnp.bfloat16)
    kernels = kernel_weight.astype(jnp.bfloat16)
    projections = attention_weight.astype(jnp.bfloat16)
    time_low = time_weight.astype(jnp.bfloat16)
    shift_low = shift_weight.astype(jnp.bfloat16)
    outlet = outlet_weight.astype(jnp.bfloat16)
    embed = sinusoid(timesteps, width_sin).astype(jnp.bfloat16)
    hidden_pre = jnp.dot(
        embed, time_low[:width_sin], preferred_element_type=jnp.float32
    ) + small_params[15:17].reshape(-1)
    hidden = jax.nn.silu(hidden_pre).astype(jnp.bfloat16)
    time_emb = jnp.dot(
        hidden, time_low[width_sin:], preferred_element_type=jnp.float32
    ) + small_params[17:19].reshape(-1)
    time_act = jax.nn.silu(time_emb).astype(jnp.bfloat16)
    time_shift = jnp.dot(time_act, shift_low, preferred_element_type=jnp.float32) + small_params[14]
    padded_noisy = widen(noisy)
    start = conv_apply(padded_noisy, inlet) + small_params[8]
    stats_one = norm_stats(start)
    normed_one = standard(start, stats_one) * small_params[0] + small_params[4]
    padded_one = widen(jax.nn.silu(normed_one).astype(jnp.bfloat16))
    inner = conv_apply(padded_one, kernels[0]) + small_params[9] + time_shift[:, None, None, :]
    stats_two = norm_stats(inner)
    normed_two = standard(inner, stats_two) * small_params[1] + small_params[5]
    padded_two = widen((jax.nn.silu(normed_two) * dropped).astype(jnp.bfloat16))
    middle = start + conv_apply(padded_two, kernels[1]) + small_params[10]
    stats_three = norm_stats(middle)
    tokens = (standard(middle, stats_three) * small_params[2] + small_params[6]).astype(
        jnp.bfloat16
    )
    tokens = tokens.reshape(images, height * breadth, chans)
    query_rows = (
        jnp.einsum("bpc,cd->bpd", tokens, projections[0], preferred_element_type=jnp.float32)
        + small_params[11]
    ).astype(jnp.bfloat16)
    key_rows = jnp.einsum(
        "bpc,cd->bpd", tokens, projections[1], preferred_element_type=jnp.float32
    ).astype(jnp.bfloat16)
    value_rows = (
        jnp.einsum("bpc,cd->bpd", tokens, projections[2], preferred_element_type=jnp.float32)
        + small_params[12]
    ).astype(jnp.bfloat16)
    all_keys, all_values = (
        lax.all_gather(key_rows, "rows", axis=1, tiled=True),
        lax.all_gather(value_rows, "rows", axis=1, tiled=True),
    )
    attended_tokens, logsum = attend(query_rows, all_keys, all_values)
    branch = (
        jnp.einsum(
            "bpc,cd->bpd", attended_tokens, projections[3], preferred_element_type=jnp.float32
        )
        + small_params[13]
    )
    final = middle + branch.reshape(middle.shape)
    stats_four = norm_stats(final)
    normed_four = standard(final, stats_four) * small_params[3] + small_params[7]
    padded_four = widen(jax.nn.silu(normed_four).astype(jnp.bfloat16))
    predicted = jnp.einsum(
        "bhwk,ck->bhwc", gather_patches(padded_four), outlet, preferred_element_type=jnp.float32
    )
    ratio = bars / (1.0 - bars)
    snr_weight = jnp.minimum(ratio, GAMMA) / ratio
    denom = 3 * height * breadth * lax.axis_size("rows") * images * lax.axis_size("batch")
    errors = predicted - target
    loss_part = jnp.sum(snr_weight * jnp.sum(errors * errors, axis=(1, 2, 3))) / denom
    grad_pred = (2.0 * snr_weight[:, None, None, None] * errors / denom).astype(jnp.bfloat16)
    outlet_grad = jnp.einsum(
        "bhwk,bhwc->ck", gather_patches(padded_four), grad_pred, preferred_element_type=jnp.float32
    )
    grad_four = conv_input_grad(grad_pred, outlet.T) * swish_grad(normed_four)
    grad_final, gain_four, shift_four = norm_back(grad_four, final, stats_four, small_params[3])
    grad_branch = grad_final.reshape(images, height * breadth, chans)
    branch_low = grad_branch.astype(jnp.bfloat16)
    out_proj_grad = jnp.einsum(
        "bpc,bpd->cd", attended_tokens, branch_low, preferred_element_type=jnp.float32
    )
    gradient_mixed_tokens = jnp.einsum(
        "bpd,cd->bpc", branch_low, projections[3], preferred_element_type=jnp.float32
    ).astype(jnp.bfloat16)
    local_dq, part_dk, part_dv = attend_back(
        query_rows, all_keys, all_values, logsum, gradient_mixed_tokens
    )
    sum_dk, sum_dv = (
        lax.psum_scatter(
            part_dk.astype(jnp.bfloat16), "rows", scatter_dimension=1, tiled=True
        ).astype(jnp.float32),
        lax.psum_scatter(
            part_dv.astype(jnp.bfloat16), "rows", scatter_dimension=1, tiled=True
        ).astype(jnp.float32),
    )
    query_grad = local_dq.astype(jnp.bfloat16)
    key_grad = sum_dk.astype(jnp.bfloat16)
    value_grad = sum_dv.astype(jnp.bfloat16)
    projection_grads = jnp.stack(
        [
            jnp.einsum("bpc,bpd->cd", tokens, query_grad, preferred_element_type=jnp.float32),
            jnp.einsum("bpc,bpd->cd", tokens, key_grad, preferred_element_type=jnp.float32),
            jnp.einsum("bpc,bpd->cd", tokens, value_grad, preferred_element_type=jnp.float32),
            out_proj_grad,
        ]
    )
    grad_tokens = (
        jnp.einsum("bpd,cd->bpc", query_grad, projections[0], preferred_element_type=jnp.float32)
        + jnp.einsum("bpd,cd->bpc", key_grad, projections[1], preferred_element_type=jnp.float32)
        + jnp.einsum("bpd,cd->bpc", value_grad, projections[2], preferred_element_type=jnp.float32)
    )
    grad_norm_three, gain_three, shift_three = norm_back(
        grad_tokens.reshape(middle.shape), middle, stats_three, small_params[2]
    )
    grad_middle = grad_final + grad_norm_three
    middle_low = grad_middle.astype(jnp.bfloat16)
    kernel_two_grad = conv_weight_grad(padded_two, middle_low)
    grad_two = conv_input_grad(middle_low, kernels[1]) * dropped * swish_grad(normed_two)
    grad_inner, gain_two, shift_two = norm_back(grad_two, inner, stats_two, small_params[1])
    shift_time_grad = jnp.sum(grad_inner, axis=(1, 2))
    inner_low = grad_inner.astype(jnp.bfloat16)
    kernel_one_grad = conv_weight_grad(padded_one, inner_low)
    grad_one = conv_input_grad(inner_low, kernels[0]) * swish_grad(normed_one)
    grad_norm_one, gain_one, shift_one = norm_back(grad_one, start, stats_one, small_params[0])
    grad_start = grad_middle + grad_norm_one
    inlet_grad = conv_weight_grad(padded_noisy, grad_start.astype(jnp.bfloat16))
    shift_weight_grad = jnp.dot(
        time_act.astype(jnp.float32).T, shift_time_grad, precision=HIGH_PRECISION
    )
    grad_act = jnp.dot(
        shift_time_grad, shift_low.astype(jnp.float32).T, precision=HIGH_PRECISION
    ) * swish_grad(time_emb)
    time_two_grad = jnp.dot(hidden.astype(jnp.float32).T, grad_act, precision=HIGH_PRECISION)
    grad_hidden = jnp.dot(
        grad_act, time_low[width_sin:].astype(jnp.float32).T, precision=HIGH_PRECISION
    ) * swish_grad(hidden_pre)
    time_one_grad = jnp.dot(embed.astype(jnp.float32).T, grad_hidden, precision=HIGH_PRECISION)
    small_grad = jnp.concatenate(
        [
            jnp.stack(
                [
                    gain_one,
                    gain_two,
                    gain_three,
                    gain_four,
                    shift_one,
                    shift_two,
                    shift_three,
                    shift_four,
                    jnp.sum(grad_start, axis=(0, 1, 2)),
                    jnp.sum(grad_inner, axis=(0, 1, 2)),
                    jnp.sum(grad_middle, axis=(0, 1, 2)),
                    jnp.sum(query_grad.astype(jnp.float32), axis=(0, 1)),
                    jnp.sum(value_grad.astype(jnp.float32), axis=(0, 1)),
                    jnp.sum(grad_branch, axis=(0, 1)),
                    jnp.sum(shift_time_grad, axis=0),
                ]
            ),
            jnp.sum(grad_hidden, axis=0).reshape(2, chans),
            jnp.sum(grad_act, axis=0).reshape(2, chans),
        ],
        axis=0,
    )
    summed = lax.psum(
        (
            inlet_grad,
            jnp.stack([kernel_one_grad, kernel_two_grad]),
            projection_grads,
            jnp.concatenate([time_one_grad, time_two_grad], axis=0),
            shift_weight_grad,
            outlet_grad,
            small_grad,
            loss_part,
        ),
        ("batch", "rows"),
    )
    loss = summed[7]
    grads = summed[:7]
    norm = jnp.sqrt(sum((jnp.sum(item * item) for item in grads)))
    scale_factor = CLIP / jnp.maximum(norm, CLIP)
    count = adam_step[0].astype(jnp.float32)
    weight_tensors = (
        inlet_weight,
        kernel_weight,
        attention_weight,
        time_weight,
        shift_weight,
        outlet_weight,
        small_params,
    )
    states = (
        state_inlet,
        state_kernel,
        state_attention,
        state_time,
        state_shift,
        state_outlet,
        state_small,
    )
    averages = (
        average_inlet,
        average_kernel,
        average_attention,
        average_time,
        average_shift,
        average_outlet,
        average_small,
    )
    members = lax.axis_size("batch")
    mine = lax.axis_index("batch")
    results = [None] * 7
    for position in (1, 2):
        length = weight_tensors[position].shape[1] // members
        own_weight = lax.dynamic_slice_in_dim(weight_tensors[position], mine * length, length, 1)
        own_grad = lax.dynamic_slice_in_dim(grads[position], mine * length, length, 1)
        results[position] = adam(
            own_weight,
            states[position],
            averages[position],
            own_grad * scale_factor,
            RATES[position],
            count,
        )
    kernel_pair, attention_pair = (
        lax.all_gather(results[1][0], "batch", axis=2, tiled=True),
        lax.all_gather(results[2][0], "batch", axis=2, tiled=True),
    )
    results[1] = (kernel_pair, results[1][1], results[1][2])
    results[2] = (attention_pair, results[2][1], results[2][2])
    for position in (0, 3, 4, 5, 6):
        results[position] = adam(
            weight_tensors[position],
            states[position],
            averages[position],
            grads[position] * scale_factor,
            RATES[position],
            count,
        )
    return (
        results[0][0],
        results[1][0],
        results[2][0],
        results[3][0],
        results[4][0],
        results[5][0],
        results[6][0],
        results[0][1],
        results[1][1],
        results[2][1],
        results[3][1],
        results[4][1],
        results[5][1],
        results[6][1],
        results[0][2],
        results[1][2],
        results[2][2],
        results[3][2],
        results[4][2],
        results[5][2],
        results[6][2],
        loss,
        norm,
    )


def solution(mesh):
    return jax.shard_map(
        local,
        mesh=mesh,
        in_specs=(
            P("batch", None, "rows", None),
            P("batch", None, "rows", None),
            P("batch"),
            P("batch", "rows", None, None),
            P(),
            P(),
            P(),
            P(),
            P(),
            P(),
            P(),
            P(),
            P(),
            P(None, None, "batch", None),
            P(None, None, "batch", None),
            P(),
            P(),
            P(),
            P(),
            P(),
            P(None, "batch", None),
            P(None, "batch", None),
            P(),
            P(),
            P(),
            P(),
        ),
        out_specs=(
            P(),
            P(),
            P(),
            P(),
            P(),
            P(),
            P(),
            P(),
            P(None, "batch", None),
            P(None, "batch", None),
            P(),
            P(),
            P(),
            P(),
            P(),
            P(None, "batch", None),
            P(None, "batch", None),
            P(),
            P(),
            P(),
            P(),
            P(),
            P(),
        ),
        check_vma=False,
    )
```

profile of v0, /device:TPU:1, one launch (start us, length us, event | category | flops | bytes accessed | tf_op | source)
XLA Modules:
  0.0 1684.6 jit_solution(1363734799162232898)
XLA Ops:
  29.2 13.2 all-reduce.17
  53.1 14.6 collective-permute-done.2
  67.7 24.5 %collective-permute-done.3 = bf16[128,1,16,256]{3,0,2,1:T(8,128)(2,1)S(1)} collective-permute-done((bf16[128,1,16,256]{3,0,2,1:T(8,128)(2,1)S(1)}, bf16[128,1,16,256]{3,0,2,1:T(8,128)(2,1)S(1)}, u32[]{:S(2)}, u32[]{:S(2)}) %collective-permute-start.3) | collective-permute-done | bytes 1048608 | tf_op jit(solution)/shard_map/ppermute | solution.py:32
  119.4 19.6 %fusion.30 = (f32[128,256]{1,0:T(8,128)S(1)}, f32[128,256]{1,0:T(8,128)S(1)}, f32[128,4,16,256]{3,0,2,1:T(8,128)}) fusion(f32[128,256]{1,0:T(8,128)S(1)} %convolution_add_fusion.2, f32[256]{0:T(256)S(1)} %bitcast.398, bf16[128,4,16,2304]{3,0,2,1:T(8,128)(2,1)} %slice_dynamic-update-slice_fusion.24, bf16[2,2304,256]{2,1,0:T(8,128)(2,1)S(1)} %convert_element_type.242), kind=kOutput, calls=%fused_computation.94 | convolution fusion | flops 9674096640 | bytes 47711232 | tf_op jit(solution)/shard_map/bhwk,kc->bhwc/dot_general | solution.py:76
  176.6 25.5 %collective-permute-done.5 = bf16[128,1,16,256]{3,0,2,1:T(8,128)(2,1)S(1)} collective-permute-done((bf16[128,1,16,256]{3,0,2,1:T(8,128)(2,1)S(1)}, bf16[128,1,16,256]{3,0,2,1:T(8,128)(2,1)S(1)}, u32[]{:S(2)}, u32[]{:S(2)}) %collective-permute-start.5) | collective-permute-done | bytes 1048608 | tf_op jit(solution)/shard_map/ppermute | solution.py:32
  225.0 23.0 %fusion.147 = (f32[128,256]{1,0:T(8,128)S(1)}, f32[128,256]{1,0:T(8,128)S(1)}, f32[128,4,16,256]{3,0,2,1:T(8,128)}) fusion(f32[256]{0:T(256)S(1)} %bitcast.427, bf16[128,4,16,2304]{3,0,2,1:T(8,128)(2,1)} %slice_dynamic-update-slice_fusion.18, bf16[2,2304,256]{2,1,0:T(8,128)(2,1)S(1)} %convert_element_type.242, f32[128,4,16,256]{3,0,2,1:T(8,128)} %get-tuple-element.302, ...), kind=kOutput, calls=%fused_computation.403 | convolution fusion | flops 9676193792 | bytes 55969792 | tf_op jit(solution)/shard_map/bhwk,kc->bhwc/dot_general | solution.py:76
  279.8 160.4 %all-gather.5.cloned.1.call-done = bf16[128,256,256]{2,0,1:T(8,128)(2,1)} async-done(((bf16[128,64,256]{2,0,1:T(8,128)(2,1)}), bf16[128,256,256]{2,0,1:T(8,128)(2,1)}) %all-gather.5.cloned.1.call-update) | async-done | bytes 16777232 | tf_op jit(solution)/shard_map/all_gather | solution.py:287
  440.2 26.8 %multiply_reduce_fusion.15 = (f32[128,64]{1,0:T(8,128)S(1)}, f32[128,64,256]{2,1,0:T(8,128)}) fusion(bf16[128,256,256]{2,0,1:T(8,128)(2,1)} %all-gather.5.cloned.1.call-done, bf16[128,64,256]{2,0,1:T(8,128)(2,1)} %add_convert_fusion.1), kind=kOutput, calls=%fused_computation.92 | convolution fusion | flops 1077927936 | bytes 29392896 | tf_op jit(solution)/shard_map/zji,zxi->zjx/dot_general | solution.py:149
  471.7 127.8 %all-gather.7.cloned.1.call-done = bf16[128,256,256]{2,0,1:T(8,128)(2,1)} async-done(((bf16[128,64,256]{2,0,1:T(8,128)(2,1)}), bf16[128,256,256]{2,0,1:T(8,128)(2,1)}) %all-gather.7.cloned.1.call-update) | async-done | bytes 16777232 | tf_op jit(solution)/shard_map/all_gather | solution.py:288
  599.4 19.2 %fusion.74 = bf16[128,64,256]{2,1,0:T(8,128)(2,1)S(1)} fusion(bf16[128,256,256]{2,0,1:T(8,128)(2,1)} %all-gather.7.cloned.1.call-done, f32[128,64,256]{2,1,0:T(8,128)} %get-tuple-element.306, f32[128,64]{1,0:T(8,128)S(1)} %fusion.19, f32[128,64]{1,0:T(8,128)S(1)} %get-tuple-element.305), kind=kOutput, calls=%fused_computation.179 | convolution fusion | flops 1084227584 | bytes 29425664 | tf_op jit(solution)/shard_map/pvg,pgj->pvj/dot_general | solution.py:156
  655.1 16.9 %collective-permute-done.6 = bf16[128,1,16,256]{3,0,2,1:T(8,128)(2,1)S(1)} collective-permute-done((bf16[128,1,16,256]{3,0,2,1:T(8,128)(2,1)}, bf16[128,1,16,256]{3,0,2,1:T(8,128)(2,1)S(1)}, u32[]{:S(2)}, u32[]{:S(2)}) %collective-permute-start.6) | collective-permute-done | bytes 1048608 | tf_op jit(solution)/shard_map/ppermute | solution.py:29
  672.0 25.0 %collective-permute-done.7 = bf16[128,1,16,256]{3,0,2,1:T(8,128)(2,1)S(1)} collective-permute-done((bf16[128,1,16,256]{3,0,2,1:T(8,128)(2,1)}, bf16[128,1,16,256]{3,0,2,1:T(8,128)(2,1)S(1)}, u32[]{:S(2)}, u32[]{:S(2)}) %collective-permute-start.7) | collective-permute-done | bytes 1048608 | tf_op jit(solution)/shard_map/ppermute | solution.py:32
  725.9 16.4 fusion.130
  785.1 14.8 convolution_convert_fusion
  800.0 24.5 %multiply_reduce_fusion.6 = (f32[128,64]{1,0:T(8,128)S(1)}, f32[128,64,256]{2,1,0:T(8,128)}) fusion(f32[128,64,256]{2,1,0:T(8,128)} %get-tuple-element.306, f32[128,64]{1,0:T(8,128)S(1)} %log_add_fusion, bf16[128,256,256]{2,0,1:T(8,128)(2,1)} %all-gather.7.cloned.1.call-done, bf16[128,64,256]{2,0,1:T(8,128)(2,1)} %convolution_convert_fusion.1), kind=kOutput, calls=%fused_computation.43 | convolution fusion | flops 1082122240 | bytes 37814272 | tf_op jit(solution)/shard_map/zji,zxi->zjx/dot_general | solution.py:169
  834.5 13.8 multiply_convert_fusion
  856.5 15.3 convolution_bitcast_fusion.2
  871.8 24.6 %convert_reduce_fusion.1 = (f32[256]{0:T(256)}, bf16[128,64,256]{2,1,0:T(8,128)(2,1)}) fusion(bf16[128,64,256]{2,1,0:T(8,128)(2,1)} %multiply_convert_fusion.2, bf16[128,256,256]{2,0,1:T(8,128)(2,1)} %all-gather.5.cloned.1.call-done), kind=kOutput, calls=%fused_computation.28 | convolution fusion | flops 1082130176 | bytes 25166848 | tf_op jit(solution)/shard_map/pvg,pgj->pvj/dot_general | solution.py:186
  905.2 18.8 %fusion.92 = f32[1,256,256]{2,1,0:T(8,128)S(1)} fusion(bf16[128,64,256]{2,1,0:T(8,128)(2,1)S(1)} %copy-done.19, f32[128,64,256]{2,0,1:T(8,128)} %bitcast.353, f32[128,64,256]{2,0,1:T(8,128)} %bitcast.366, f32[128,256]{1,0:T(8,128)S(1)} %copy.380, f32[128,256]{1,0:T(8,128)S(1)} %copy.373, f32[128,256]{1,0:T(8,128)S(1)} %copy.371, f32[128,256]{1,0:T(8,128)S(1)} %copy.378), kind=kOutput, calls=%fused_computation.203 | convolution fusion | flops 1090519040 | bytes 21757952 | tf_op jit(solution)/shard_map/bpc,bpd->cd/dot_general | solution.py:317
  924.1 39.1 %reduce-scatter.5.cloned.1.call-done = bf16[128,64,256]{2,1,0:T(8,128)(2,1)} async-done(((bf16[128,256,256]{2,1,0:T(8,128)(2,1)}), bf16[128,64,256]{2,1,0:T(8,128)(2,1)}) %reduce-scatter.5.cloned.1.call-update) | async-done | bytes 4194320 | tf_op jit(solution)/shard_map/reduce_scatter | solution.py:330
  973.6 146.3 %reduce-scatter.3.cloned.1.call-done = bf16[128,64,256]{2,1,0:T(8,128)(2,1)} async-done(((bf16[128,256,256]{2,1,0:T(8,128)(2,1)}), bf16[128,64,256]{2,1,0:T(8,128)(2,1)}) %reduce-scatter.3.cloned.1.call-update) | async-done | bytes 4194320 | tf_op jit(solution)/shard_map/reduce_scatter | solution.py:327
  1130.4 15.2 multiply_reduce_fusion.12
  1157.5 17.2 %fusion.160 = (bf16[128,4,16,256]{3,0,2,1:T(8,128)(2,1)S(1)}, f32[128,4,16,256]{3,0,2,1:T(8,128)}, f32[256]{0:T(256)}) fusion(f32[128,4,16,256]{3,0,2,1:T(8,128)} %copy-done.5, f32[128,256]{1,0:T(8,128)S(1)} %copy.394, f32[128,256]{1,0:T(8,128)S(1)} %copy-done.28, f32[128,4,16,256]{3,0,2,1:T(8,128)} %get-tuple-element.304, f32[128,256]{1,0:T(8,128)S(1)} %copy-done.26, ...), kind=kLoop, calls=%fused_computation.406 | loop fusion | flops 25165568 | bytes 46663680 | tf_op jit(solution)/shard_map/convert_element_type | solution.py:354
  1174.7 17.1 %convolution_bitcast_fusion = f32[1,2304,256]{2,1,0:T(8,128)} fusion(bf16[128,4,16,2304]{3,0,2,1:T(8,128)(2,1)} %slice_dynamic-update-slice_fusion.18, bf16[128,4,16,256]{3,0,2,1:T(8,128)(2,1)S(1)} %get-tuple-element.245), kind=kOutput, calls=%fused_computation.160 | convolution fusion | flops 9663676416 | bytes 44302336 | tf_op jit(solution)/shard_map/bhwk,bhwc->kc/dot_general | solution.py:82
  1213.0 25.0 %collective-permute-done.11 = bf16[128,1,16,256]{3,0,2,1:T(8,128)(2,1)S(1)} collective-permute-done((bf16[128,1,16,256]{3,0,2,1:T(8,128)(2,1)S(1)}, bf16[128,1,16,256]{3,0,2,1:T(8,128)(2,1)S(1)}, u32[]{:S(2)}, u32[]{:S(2)}) %collective-permute-start.11) | collective-permute-done | bytes 1048608 | tf_op jit(solution)/shard_map/ppermute | solution.py:32
  1262.1 25.5 %multiply_reduce_fusion.2 = (f32[256]{0:T(256)S(1)}, f32[128,256]{1,0:T(8,128)S(1)}, f32[128,256]{1,0:T(8,128)S(1)}, f32[256]{0:T(256)S(1)}, f32[128,4,16,256]{3,0,2,1:T(8,128)}) fusion(f32[128,256]{1,0:T(8,128)S(1)} %copy-done.36, f32[128,256]{1,0:T(8,128)S(1)} %copy-done.34, f32[128,256]{1,0:T(8,128)S(1)} %copy-done.45, ...), kind=kOutput, calls=%fused_computation.31 | convolution fusion | flops 9713942528 | bytes 64754688 | tf_op jit(solution)/shard_map/bhwk,kc->bhwc/dot_general | solution.py:76
  1309.0 17.2 %convolution_bitcast_fusion.1 = f32[1,2304,256]{2,1,0:T(8,128)} fusion(bf16[128,4,16,2304]{3,0,2,1:T(8,128)(2,1)} %slice_dynamic-update-slice_fusion.24, bf16[128,4,16,256]{3,0,2,1:T(8,128)(2,1)S(1)} %get-tuple-element.242), kind=kOutput, calls=%fused_computation.161 | convolution fusion | flops 9663676416 | bytes 44302336 | tf_op jit(solution)/shard_map/bhwk,bhwc->kc/dot_general | solution.py:82
  1343.7 35.3 %collective-permute-done.13 = bf16[128,1,16,256]{3,0,2,1:T(8,128)(2,1)S(1)} collective-permute-done((bf16[128,1,16,256]{3,0,2,1:T(8,128)(2,1)}, bf16[128,1,16,256]{3,0,2,1:T(8,128)(2,1)S(1)}, u32[]{:S(2)}, u32[]{:S(2)}) %collective-permute-start.13) | collective-permute-done | bytes 1048608 | tf_op jit(solution)/shard_map/ppermute | solution.py:32
  1404.6 23.4 %multiply_reduce_fusion.3 = (f32[256]{0:T(256)S(1)}, f32[128,256]{1,0:T(8,128)S(1)}, f32[128,256]{1,0:T(8,128)S(1)}, f32[256]{0:T(256)S(1)}, f32[128,4,16,256]{3,0,2,1:T(8,128)}) fusion(f32[128,256]{1,0:T(8,128)S(1)} %copy-done.24, f32[128,256]{1,0:T(8,128)S(1)} %copy-done.22, f32[128,4,16,256]{3,0,2,1:T(8,128)} %get-tuple-element.302, ...), kind=kOutput, calls=%fused_computation.32 | convolution fusion | flops 9705553920 | bytes 56235008 | tf_op jit(solution)/shard_map/bhwk,kc->bhwc/dot_general | solution.py:76
  1439.4 12.4 fusion.159
  1455.1 59.4 %all-reduce.22 = (f32[27,256]{1,0:T(8,128)S(1)}, f32[3,2304]{1,0:T(4,128)S(1)}, f32[19,256]{1,0:T(8,128)S(1)}, f32[]{:T(128)}) all-reduce(f32[27,256]{1,0:T(8,128)S(1)} %fusion.95, f32[3,2304]{1,0:T(4,128)S(1)} %copy-done.51, f32[19,256]{1,0:T(8,128)S(1)} %concatenate.128, ...), channel_id=1, replica_groups=mesh['batch'=8,'rows'=4] {'batch','rows'}, use_global_device_ids=true, to_apply=%region_56.57 | all-reduce | flops 18689 | bytes 149512 | tf_op jit(solution)/shard_map/psum | solution.py:402
  1574.4 92.5 %all-gather.9.cloned.1.call-done = f32[2,2,2304,256]{3,2,1,0:T(8,128)} async-done(((f32[2,2,288,256]{3,2,1,0:T(8,128)}), f32[2,2,2304,256]{3,2,1,0:T(8,128)}) %all-gather.9.cloned.1.call-update) | async-done | bytes 9437200 | tf_op jit(solution)/shard_map/all_gather | solution.py:463
  (501 shorter events, 510.6 us)
Async XLA Ops:
  7.2 433.0 %all-gather.5.cloned.1.call-start = ((), (), s32[]{:S(2)}) async-start(), calls=%async_computation.2 | async-start | bytes 20971520 | tf_op jit(solution)/shard_map/all_gather | solution.py:287
  9.7 12.6 collective-permute-start
  13.7 8.6 collective-permute-start.1
  16.6 134.2 %copy-start.74 = (f32[1,256]{1,0:T(1,128)}, f32[1,256]{1,0:T(1,128)S(1)}, u32[]{:S(2)}) copy-start(f32[1,256]{1,0:T(1,128)S(1)} %get-tuple-element.281) | copy-start | bytes 3076
  16.6 134.2 %copy-start.76 = (f32[1,256]{1,0:T(1,128)}, f32[1,256]{1,0:T(1,128)S(1)}, u32[]{:S(2)}) copy-start(f32[1,256]{1,0:T(1,128)S(1)} %get-tuple-element.283) | copy-start | bytes 3076
  16.6 134.2 %copy-start.81 = (f32[1,256]{1,0:T(1,128)}, f32[1,256]{1,0:T(1,128)S(1)}, u32[]{:S(2)}) copy-start(f32[1,256]{1,0:T(1,128)S(1)} %get-tuple-element.280) | copy-start | bytes 3076
  16.6 208.4 %copy-start.64 = (f32[1,256]{1,0:T(1,128)}, f32[1,256]{1,0:T(1,128)S(1)}, u32[]{:S(2)}) copy-start(f32[1,256]{1,0:T(1,128)S(1)} %get-tuple-element.286) | copy-start | bytes 3076
  16.6 242.2 %copy-start.68 = (f32[1,256]{1,0:T(1,128)}, f32[1,256]{1,0:T(1,128)S(1)}, u32[]{:S(2)}) copy-start(f32[1,256]{1,0:T(1,128)S(1)} %get-tuple-element.278) | copy-start | bytes 3076
  22.3 202.7 %copy-start.10 = (bf16[2,2304,256]{2,1,0:T(8,128)(2,1)}, bf16[2,2304,256]{2,1,0:T(8,128)(2,1)S(1)}, u32[]{:S(2)}) copy-start(bf16[2,2304,256]{2,1,0:T(8,128)(2,1)S(1)} %convert_element_type.242) | copy-start | bytes 7077892
  48.2 19.5 %collective-permute-start.2 = (bf16[128,1,16,256]{3,0,2,1:T(8,128)(2,1)S(1)}, bf16[128,1,16,256]{3,0,2,1:T(8,128)(2,1)S(1)}, u32[]{:S(2)}, u32[]{:S(2)}) collective-permute-start(bf16[128,1,16,256]{3,0,2,1:T(8,128)(2,1)S(1)} %get-tuple-element.259), channel_id=1, source_target_pairs={{0,1},{1,2},{2,3},{4,5},{5,6},{6,7},{8,9},{9,10},{10,11},{12,13},{... | collective-permute-start | bytes 3145736 | tf_op jit(solution)/shard_map/ppermute | solution.py:29
  50.3 41.9 %collective-permute-start.3 = (bf16[128,1,16,256]{3,0,2,1:T(8,128)(2,1)S(1)}, bf16[128,1,16,256]{3,0,2,1:T(8,128)(2,1)S(1)}, u32[]{:S(2)}, u32[]{:S(2)}) collective-permute-start(bf16[128,1,16,256]{3,0,2,1:T(8,128)(2,1)S(1)} %get-tuple-element.260), channel_id=1, source_target_pairs={{1,0},{2,1},{3,2},{5,4},{6,5},{7,6},{9,8},{10,9},{11,10},{13,12},{... | collective-permute-start | bytes 3145736 | tf_op jit(solution)/shard_map/ppermute | solution.py:32
  53.1 97.7 %copy-start.44 = (f32[128,256]{1,0:T(8,128)}, f32[128,256]{1,0:T(8,128)S(1)}, u32[]{:S(2)}) copy-start(f32[128,256]{1,0:T(8,128)S(1)} %convolution_add_fusion.2) | copy-start | bytes 393220
  161.5 15.0 collective-permute-start.4
  163.5 38.5 %collective-permute-start.5 = (bf16[128,1,16,256]{3,0,2,1:T(8,128)(2,1)S(1)}, bf16[128,1,16,256]{3,0,2,1:T(8,128)(2,1)S(1)}, u32[]{:S(2)}, u32[]{:S(2)}) collective-permute-start(bf16[128,1,16,256]{3,0,2,1:T(8,128)(2,1)S(1)} %get-tuple-element.258), channel_id=1, source_target_pairs={{1,0},{2,1},{3,2},{5,4},{6,5},{7,6},{9,8},{10,9},{11,10},{13,12},{... | collective-permute-start | bytes 3145736 | tf_op jit(solution)/shard_map/ppermute | solution.py:32
  268.9 330.6 %all-gather.7.cloned.1.call-start = ((), (), s32[]{:S(2)}) async-start(), calls=%async_computation.3 | async-start | bytes 20971520 | tf_op jit(solution)/shard_map/all_gather | solution.py:288
  274.3 688.8 %reduce-scatter.5.cloned.1.call-start = ((), (), s32[]{:S(2)}) async-start(), calls=%async_computation.5 | async-start | bytes 20971520 | tf_op jit(solution)/shard_map/reduce_scatter | solution.py:330
  471.7 147.0 %copy-start.84 = (f32[1,256]{1,0:T(1,128)S(1)}, f32[1,256]{1,0:T(1,128)}, u32[]{:S(2)}) copy-start(f32[1,256]{1,0:T(1,128)} %get-tuple-element.274) | copy-start | bytes 3076
  651.2 20.7 %collective-permute-start.6 = (bf16[128,1,16,256]{3,0,2,1:T(8,128)(2,1)}, bf16[128,1,16,256]{3,0,2,1:T(8,128)(2,1)S(1)}, u32[]{:S(2)}, u32[]{:S(2)}) collective-permute-start(bf16[128,1,16,256]{3,0,2,1:T(8,128)(2,1)} %get-tuple-element.255), channel_id=1, source_target_pairs={{0,1},{1,2},{2,3},{4,5},{5,6},{6,7},{8,9},{9,10},{10,11},{12,13},{... | collective-permute-start | bytes 3145736 | tf_op jit(solution)/shard_map/ppermute | solution.py:29
  653.5 43.4 %collective-permute-start.7 = (bf16[128,1,16,256]{3,0,2,1:T(8,128)(2,1)}, bf16[128,1,16,256]{3,0,2,1:T(8,128)(2,1)S(1)}, u32[]{:S(2)}, u32[]{:S(2)}) collective-permute-start(bf16[128,1,16,256]{3,0,2,1:T(8,128)(2,1)} %get-tuple-element.256), channel_id=1, source_target_pairs={{1,0},{2,1},{3,2},{5,4},{6,5},{7,6},{9,8},{10,9},{11,10},{13,12},{... | collective-permute-start | bytes 3145736 | tf_op jit(solution)/shard_map/ppermute | solution.py:32
  743.0 3.5 collective-permute-start.8
  745.2 4.4 collective-permute-start.9
  800.0 320.0 %reduce-scatter.3.cloned.1.call-start = ((), (), s32[]{:S(2)}) async-start(), calls=%async_computation.4 | async-start | bytes 20971520 | tf_op jit(solution)/shard_map/reduce_scatter | solution.py:327
  848.4 678.7 %all-reduce.21.cloned.1.call-start = ((), (), s32[]{:S(2)}) async-start(), calls=%async_computation.8 | async-start | bytes 15204352 | tf_op jit(solution)/shard_map/psum | solution.py:402
  963.2 167.3 %copy-start.28 = (f32[128,256]{1,0:T(8,128)S(1)}, f32[128,256]{1,0:T(8,128)}, u32[]{:S(2)}) copy-start(f32[128,256]{1,0:T(8,128)} %copy-done.27) | copy-start | bytes 393220
  963.2 167.3 %copy-start.69 = (f32[1,256]{1,0:T(1,128)S(1)}, f32[1,256]{1,0:T(1,128)}, u32[]{:S(2)}) copy-start(f32[1,256]{1,0:T(1,128)} %copy-done.68) | copy-start | bytes 3076
  973.6 156.8 %copy-start.26 = (f32[128,256]{1,0:T(8,128)S(1)}, f32[128,256]{1,0:T(8,128)}, u32[]{:S(2)}) copy-start(f32[128,256]{1,0:T(8,128)} %copy-done.25) | copy-start | bytes 393220
  1192.1 21.0 %collective-permute-start.10 = (bf16[128,1,16,256]{3,0,2,1:T(8,128)(2,1)S(1)}, bf16[128,1,16,256]{3,0,2,1:T(8,128)(2,1)S(1)}, u32[]{:S(2)}, u32[]{:S(2)}) collective-permute-start(bf16[128,1,16,256]{3,0,2,1:T(8,128)(2,1)S(1)} %get-tuple-element.253), channel_id=1, source_target_pairs={{0,1},{1,2},{2,3},{4,5},{5,6},{6,7},{8,9},{9,10},{10,11},{12,13},{... | collective-permute-start | bytes 3145736 | tf_op jit(solution)/shard_map/ppermute | solution.py:29
  1194.8 43.1 %collective-permute-start.11 = (bf16[128,1,16,256]{3,0,2,1:T(8,128)(2,1)S(1)}, bf16[128,1,16,256]{3,0,2,1:T(8,128)(2,1)S(1)}, u32[]{:S(2)}, u32[]{:S(2)}) collective-permute-start(bf16[128,1,16,256]{3,0,2,1:T(8,128)(2,1)S(1)} %get-tuple-element.254), channel_id=1, source_target_pairs={{1,0},{2,1},{3,2},{5,4},{6,5},{7,6},{9,8},{10,9},{11,10},{13,12},{... | collective-permute-start | bytes 3145736 | tf_op jit(solution)/shard_map/ppermute | solution.py:32
  1327.7 16.0 collective-permute-start.12
  1329.8 49.2 %collective-permute-start.13 = (bf16[128,1,16,256]{3,0,2,1:T(8,128)(2,1)}, bf16[128,1,16,256]{3,0,2,1:T(8,128)(2,1)S(1)}, u32[]{:S(2)}, u32[]{:S(2)}) collective-permute-start(bf16[128,1,16,256]{3,0,2,1:T(8,128)(2,1)} %get-tuple-element.252), channel_id=1, source_target_pairs={{1,0},{2,1},{3,2},{5,4},{6,5},{7,6},{9,8},{10,9},{11,10},{13,12},{... | collective-permute-start | bytes 3145736 | tf_op jit(solution)/shard_map/ppermute | solution.py:32
  1339.7 234.6 %all-gather.11.cloned.1.call-start = ((), (), s32[]{:S(2)}) async-start(), calls=%async_computation.7 | async-start | bytes 2359296 | tf_op jit(solution)/shard_map/all_gather | solution.py:464
  1544.6 122.3 %all-gather.9.cloned.1.call-start = ((), (), s32[]{:S(2)}) async-start(), calls=%async_computation.6 | async-start | bytes 10616832 | tf_op jit(solution)/shard_map/all_gather | solution.py:463
  (89 other events, 1581.5 us)
Sparse Core Ops, SparseCore 0:
  269.0 171.1 all-gather.4
  442.0 157.4 all-gather.6
  800.1 163.0 reduce-scatter.4
  966.1 153.8 reduce-scatter.2
  1339.9 187.1 all-reduce.20
  1544.7 29.5 all-gather.10
  1576.6 90.2 all-gather.8
where the time goes:
time: 1690 us; the launch traced here: 1680 us
  waiting for transfers between devices  775 us (46%)
  matrix products  409 us (24%)
  other arithmetic  177 us (10%)
  blocking collectives  151 us (9%)
  local copies, waits for them, and re-layouts  121 us (7%)
  starting transfers between devices  27.5 us (2%)
  between operations  23.7 us (1%)
    all_gather x1, waiting for transfers between devices, local(): lax.all_gather(key_rows, 'rows', axis=1, tiled=True)  160 us
    reduce_scatter x1, waiting for transfers between devices, local(): lax.psum_scatter(part_dk.astype(jnp.bfloat16), 'rows', scatter_dimension=...  146 us
    ppermute x7, waiting for transfers between devices, padded_2(): lax.ppermute(lax.slice_in_dim(block, 0, width, axis=dim), axis, backward)  138 us
    all_gather x1, waiting for transfers between devices, local(): lax.all_gather(value_rows, 'rows', axis=1, tiled=True)  128 us
    dot_general x6, matrix products, conv_apply(): jnp.einsum('bhwk,kc->bhwc', gather_patches(padded), weight, preferred_ele...  105 us
    unnamed x248, local copies, waits for them, and re-layouts  94.6 us
    all_gather x1, waiting for transfers between devices, local(): lax.all_gather(results[1][0], 'batch', axis=2, tiled=True)  92.5 us
    psum x1, blocking collectives, local(): lax.psum((inlet_grad, jnp.stack([kernel_one_grad, kernel_two_grad]), proj...  59.4 us
  transfers between devices with their start and end apart: 21, of which 18 were waited for; matrix products, arithmetic and copies ran while one was open for 17% of the time, Pallas kernels for 0%

commit v1 on v0

--- a/solution.py
+++ b/solution.py
@@ -2,6 +2,7 @@
 
 import jax
 import jax.numpy as jnp
+import numpy as np
 from jax import lax
 from jax.sharding import PartitionSpec as P
 
@@ -21,25 +22,14 @@
 RATES = (0.1, 0.01, 0.03, 0.05, 0.02, 0.01, 0.2)
 
 
-def padded_2(block, sides, width):
-    for axis, dim in sides:
-        count = lax.axis_size(axis)
-        forward = [(i, i + 1) for i in range(count - 1)]
-        backward = [(target, source) for source, target in forward]
-        low = lax.ppermute(
-            lax.slice_in_dim(block, block.shape[dim] - width, None, axis=dim), axis, forward
-        )
-        high = lax.ppermute(lax.slice_in_dim(block, 0, width, axis=dim), axis, backward)
-        block = jnp.concatenate([low, block, high], axis=dim)
-    return block
+def bar_table():
+    beta_rates = 0.0001 + (0.02 - 0.0001) * np.arange(1000, dtype=np.float64) / 999.0
+    return np.exp(np.cumsum(np.log(1.0 - beta_rates))).astype(np.float32)
 
 
 def alpha_bars(timesteps):
-    steps_all = jnp.arange(1000).astype(jnp.float32)
-    beta_rates = 0.0001 + (0.02 - 0.0001) * steps_all / 999.0
-    bar_table = jnp.exp(jnp.cumsum(jnp.log(1.0 - beta_rates)))
     one_hot = (timesteps[:, None] == jnp.arange(1000)[None, :]).astype(jnp.float32)
-    return jnp.sum(one_hot * bar_table[None, :], axis=1)
+    return jnp.sum(one_hot * bar_table()[None, :], axis=1)
 
 
 def sinusoid(timesteps, width):
@@ -49,39 +39,26 @@
     return jnp.concatenate([jnp.sin(angles), jnp.cos(angles)], axis=1)
 
 
-def widen(field):
-    padded = padded_2(field, (("rows", 1),), 1)
-    return jnp.pad(padded, ((0, 0), (0, 0), (1, 1), (0, 0)))
-
-
-def widen_back(field):
-    padded = padded_2(field, (("rows", 1),), 1)
-    return jnp.pad(padded, ((0, 0), (0, 0), (1, 1), (0, 0)))
-
-
-def gather_patches(padded):
-    height = padded.shape[1] - 2
-    breadth = padded.shape[2] - 2
-    return jnp.concatenate(
-        [
-            padded[:, row_off : row_off + height, col_off : col_off + breadth, :]
-            for row_off in range(3)
-            for col_off in range(3)
-        ],
-        axis=3,
-    )
-
-
-def conv_apply(padded, weight):
-    return jnp.einsum(
-        "bhwk,kc->bhwc", gather_patches(padded), weight, preferred_element_type=jnp.float32
-    )
-
-
-def conv_weight_grad(padded, grad_out):
-    return jnp.einsum(
-        "bhwk,bhwc->kc", gather_patches(padded), grad_out, preferred_element_type=jnp.float32
-    )
+DIMS = ("NHWC", "HWIO", "NHWC")
+
+
+def conv_apply(field, weight):
+    kernel = weight.reshape(3, 3, -1, weight.shape[1])
+    return lax.conv_general_dilated(
+        field, kernel, (1, 1), "SAME", dimension_numbers=DIMS, preferred_element_type=jnp.float32
+    )
+
+
+def conv_weight_grad(field, grad_out):
+    out = lax.conv_general_dilated(
+        field,
+        grad_out,
+        (1, 1),
+        ((1, 1), (1, 1)),
+        dimension_numbers=("CHWN", "IHWO", "HWNC"),
+        preferred_element_type=jnp.float32,
+    )
+    return out.reshape(-1, grad_out.shape[3])
 
 
 def conv_input_grad(grad_out, weight):
@@ -90,7 +67,7 @@
     flipped = jnp.transpose(weight.reshape(9, inputs, outputs)[::-1], (0, 2, 1)).reshape(
         9 * outputs, inputs
     )
-    return conv_apply(widen_back(grad_out), flipped)
+    return conv_apply(grad_out, flipped)
 
 
 def grouped_view(field):
@@ -102,11 +79,6 @@
     total = jnp.sum(grouped, axis=(1, 3))
     square = jnp.sum(grouped * grouped, axis=(1, 3))
     count = grouped.shape[1] * grouped.shape[3]
-    total, square = (
-        lax.psum(total.astype(jnp.bfloat16), "rows").astype(jnp.float32),
-        lax.psum(square.astype(jnp.bfloat16), "rows").astype(jnp.float32),
-    )
-    count = count * lax.axis_size("rows")
     mean = total / count
     return (mean, lax.rsqrt(square / count - mean * mean + EPS_NORM))
 
@@ -127,11 +99,6 @@
     first_sum = jnp.sum(scaled, axis=(1, 3))
     second_sum = jnp.sum(scaled * grouped, axis=(1, 3))
     count = grouped.shape[1] * grouped.shape[3]
-    first_sum, second_sum = (
-        lax.psum(first_sum.astype(jnp.bfloat16), "rows").astype(jnp.float32),
-        lax.psum(second_sum.astype(jnp.bfloat16), "rows").astype(jnp.float32),
-    )
-    count = count * lax.axis_size("rows")
     input_grad = (
         scaled
         - first_sum[:, None, :, None] / count
@@ -234,6 +201,12 @@
 ):
     chans = kernel_weight.shape[2]
     width_sin = time_weight.shape[0] - time_weight.shape[1]
+    rows = lax.axis_size("rows")
+    own = timesteps.shape[0] // rows
+    timesteps = lax.dynamic_slice_in_dim(timesteps, lax.axis_index("rows") * own, own, 0)
+    x_clean = lax.all_to_all(x_clean, "rows", 0, 2, tiled=True)
+    noise = lax.all_to_all(noise, "rows", 0, 2, tiled=True)
+    keep_mask = lax.all_to_all(keep_mask.astype(jnp.bfloat16), "rows", 0, 1, tiled=True)
     bars = alpha_bars(timesteps)
     level = bars[:, None, None, None]
     clean = jnp.transpose(x_clean, (0, 2, 3, 1))
@@ -257,15 +230,15 @@
     ) + small_params[17:19].reshape(-1)
     time_act = jax.nn.silu(time_emb).astype(jnp.bfloat16)
     time_shift = jnp.dot(time_act, shift_low, preferred_element_type=jnp.float32) + small_params[14]
-    padded_noisy = widen(noisy)
+    padded_noisy = noisy
     start = conv_apply(padded_noisy, inlet) + small_params[8]
     stats_one = norm_stats(start)
     normed_one = standard(start, stats_one) * small_params[0] + small_params[4]
-    padded_one = widen(jax.nn.silu(normed_one).astype(jnp.bfloat16))
+    padded_one = jax.nn.silu(normed_one).astype(jnp.bfloat16)
     inner = conv_apply(padded_one, kernels[0]) + small_params[9] + time_shift[:, None, None, :]
     stats_two = norm_stats(inner)
     normed_two = standard(inner, stats_two) * small_params[1] + small_params[5]
-    padded_two = widen((jax.nn.silu(normed_two) * dropped).astype(jnp.bfloat16))
+    padded_two = (jax.nn.silu(normed_two) * dropped).astype(jnp.bfloat16)
     middle = start + conv_apply(padded_two, kernels[1]) + small_params[10]
     stats_three = norm_stats(middle)
     tokens = (standard(middle, stats_three) * small_params[2] + small_params[6]).astype(
@@ -283,10 +256,7 @@
         jnp.einsum("bpc,cd->bpd", tokens, projections[2], preferred_element_type=jnp.float32)
         + small_params[12]
     ).astype(jnp.bfloat16)
-    all_keys, all_values = (
-        lax.all_gather(key_rows, "rows", axis=1, tiled=True),
-        lax.all_gather(value_rows, "rows", axis=1, tiled=True),
-    )
+    all_keys, all_values = key_rows, value_rows
     attended_tokens, logsum = attend(query_rows, all_keys, all_values)
     branch = (
         jnp.einsum(
@@ -297,19 +267,15 @@
     final = middle + branch.reshape(middle.shape)
     stats_four = norm_stats(final)
     normed_four = standard(final, stats_four) * small_params[3] + small_params[7]
-    padded_four = widen(jax.nn.silu(normed_four).astype(jnp.bfloat16))
-    predicted = jnp.einsum(
-        "bhwk,ck->bhwc", gather_patches(padded_four), outlet, preferred_element_type=jnp.float32
-    )
+    padded_four = jax.nn.silu(normed_four).astype(jnp.bfloat16)
+    predicted = conv_apply(padded_four, outlet.T)
     ratio = bars / (1.0 - bars)
     snr_weight = jnp.minimum(ratio, GAMMA) / ratio
     denom = 3 * height * breadth * lax.axis_size("rows") * images * lax.axis_size("batch")
     errors = predicted - target
     loss_part = jnp.sum(snr_weight * jnp.sum(errors * errors, axis=(1, 2, 3))) / denom
     grad_pred = (2.0 * snr_weight[:, None, None, None] * errors / denom).astype(jnp.bfloat16)
-    outlet_grad = jnp.einsum(
-        "bhwk,bhwc->ck", gather_patches(padded_four), grad_pred, preferred_element_type=jnp.float32
-    )
+    outlet_grad = conv_weight_grad(padded_four, grad_pred).T
     grad_four = conv_input_grad(grad_pred, outlet.T) * swish_grad(normed_four)
     grad_final, gain_four, shift_four = norm_back(grad_four, final, stats_four, small_params[3])
     grad_branch = grad_final.reshape(images, height * breadth, chans)
@@ -323,14 +289,7 @@
     local_dq, part_dk, part_dv = attend_back(
         query_rows, all_keys, all_values, logsum, gradient_mixed_tokens
     )
-    sum_dk, sum_dv = (
-        lax.psum_scatter(
-            part_dk.astype(jnp.bfloat16), "rows", scatter_dimension=1, tiled=True
-        ).astype(jnp.float32),
-        lax.psum_scatter(
-            part_dv.astype(jnp.bfloat16), "rows", scatter_dimension=1, tiled=True
-        ).astype(jnp.float32),
-    )
+    sum_dk, sum_dv = part_dk, part_dv
     query_grad = local_dq.astype(jnp.bfloat16)
     key_grad = sum_dk.astype(jnp.bfloat16)
     value_grad = sum_dv.astype(jnp.bfloat16)

time: 1690 us -> 1060 us (0.63)
  waiting for transfers between devices: 775 us -> 202 us
  blocking collectives: 151 us -> 43 us
  matrix products: 409 us -> 516 us
  local copies, waits for them, and re-layouts: 121 us -> 71.3 us
  Pallas kernels: 0 us -> 25.9 us
  other arithmetic: 177 us -> 157 us
    conv_general_dilated x0 -> x11, matrix products: none -> 412 us  [the longest x4 303 us: conv_weight_grad(): lax.conv_general_dilated(field, grad_out, (1, 1), ((1, 1), (1, 1)), dimen...]
    all_gather x2 -> x0, waiting for transfers between devices: 288 us -> none  [the longest x1 160 us: local(): lax.all_gather(key_rows, 'rows', axis=1, tiled=True)]
    dot_general x12 -> x0, matrix products: 193 us -> none  [the longest x6 105 us: conv_apply(): jnp.einsum('bhwk,kc->bhwc', gather_patches(padded), weight, preferred_ele...]
    ppermute x14 -> x0, waiting for transfers between devices: 186 us -> none  [the longest x7 138 us: padded_2(): lax.ppermute(lax.slice_in_dim(block, 0, width, axis=dim), axis, backward)]
    reduce_scatter x2 -> x0, waiting for transfers between devices: 185 us -> none  [the longest x1 146 us: local(): lax.psum_scatter(part_dk.astype(jnp.bfloat16), 'rows', scatter_dimension=...]
    psum x8 -> x0, blocking collectives: 91.2 us -> none  [the longest x4 46.3 us: norm_stats(): lax.psum(square.astype(jnp.bfloat16), 'rows').astype(jnp.float32)]
    psum x1, waiting for transfers between devices: 10.7 us -> 86.1 us  [local(): lax.psum((inlet_grad, jnp.stack([kernel_one_grad, kernel_two_grad]), proj...]
    unnamed x248 -> x246, local copies, waits for them, and re-layouts: 94.6 us -> 31.9 us
  transfers between devices with their start and end apart: 21 -> 6, of which waited for: 18 -> 4; matrix products, arithmetic and copies ran while one was open for 17% -> 12% of each run, Pallas kernels for 0% -> 0%
where the time goes in v1:
time: 1060 us; the launch traced here: 1050 us
  matrix products  516 us (49%)
  waiting for transfers between devices  202 us (19%)
  other arithmetic  157 us (15%)
  local copies, waits for them, and re-layouts  71.3 us (7%)
  blocking collectives  43 us (4%)
  Pallas kernels  25.9 us (2%)
  between operations  23 us (2%)
  starting transfers between devices  13.7 us (1%)
    conv_general_dilated x4, matrix products, conv_weight_grad(): lax.conv_general_dilated(field, grad_out, (1, 1), ((1, 1), (1, 1)), dimen...  303 us
    conv_general_dilated x7, matrix products, conv_apply(): lax.conv_general_dilated(field, kernel, (1, 1), 'SAME', dimension_numbers...  109 us
    all_gather x1, waiting for transfers between devices, local(): lax.all_gather(results[1][0], 'batch', axis=2, tiled=True)  92.5 us
    psum x1, waiting for transfers between devices, local(): lax.psum((inlet_grad, jnp.stack([kernel_one_grad, kernel_two_grad]), proj...  86.1 us
    psum x1, blocking collectives, local(): lax.psum((inlet_grad, jnp.stack([kernel_one_grad, kernel_two_grad]), proj...  43 us
    unnamed x246, local copies, waits for them, and re-layouts  31.9 us
    unnamed x1, Pallas kernels  25.9 us
  transfers between devices with their start and end apart: 6, of which 4 were waited for; matrix products, arithmetic and copies ran while one was open for 12% of the time, Pallas kernels for 0%

profile of v1, /device:TPU:1, one launch (start us, length us, event | category | flops | bytes accessed | tf_op | source)
XLA Modules:
  0.0 1050.7 jit_solution(1766779443285551875)
XLA Ops:
  42.1 6.7 convert_element_type.138
  81.4 13.7 %fusion.15 = (f32[32,256]{1,0:T(8,128)S(1)}, f32[32,256]{1,0:T(8,128)S(1)}, f32[32,16,16,256]{3,0,2,1:T(8,128)}) fusion(f32[32,256]{1,0:T(8,128)S(1)} %copy-done.38, f32[256]{0:T(256)S(1)} %bitcast.382, bf16[32,16,16,256]{3,0,2,1:T(8,128)(2,1)S(1)} %multiply_convert_fusion.4, bf16[3,3,256,256]{3,2,1,0:T(8,128)(2,1)S(1)} %bitcast.350), kind=kOutput, calls=%fused_computation.67 | convolution fusion | flops 8885616640 | bytes 13861888 | tf_op jit(solution)/shard_map/conv_general_dilated | solution.py:47
  95.6 11.0 %all-to-all-done.2 = bf16[128,4,16,256]{3,2,1,0:T(8,128)(2,1)} async-done(((bf16[128,4,16,256]{3,2,1,0:T(8,128)(2,1)}), bf16[128,4,16,256]{3,2,1,0:T(8,128)(2,1)}, u32[]{:S(2)}, u32[]{:S(2)}) %all-to-all-start.2) | async-done | bytes 4194336 | tf_op jit(solution)/shard_map/all_to_all | solution.py:209
  106.6 7.0 convert_multiply_fusion
  113.7 10.0 copy.283
  128.0 16.4 %fusion.115 = (f32[32,256]{1,0:T(8,128)S(1)}, f32[32,256]{1,0:T(8,128)S(1)}, f32[32,16,16,256]{3,0,2,1:T(8,128)}) fusion(f32[256]{0:T(256)S(1)} %bitcast.411, bf16[32,16,16,256]{3,0,2,1:T(8,128)(2,1)S(1)} %fusion.4, bf16[3,3,256,256]{3,2,1,0:T(8,128)(2,1)S(1)} %bitcast.348, f32[32,16,16,256]{3,0,2,1:T(8,128)} %get-tuple-element.250, f32[256]{0:T(256)S(1)} %bitcast.376), kind=kOutput, calls=%fused_computation.274 | convolution fusion | flops 8887713792 | bytes 22218752 | tf_op jit(solution)/shard_map/conv_general_dilated | solution.py:47
  159.4 8.2 broadcast_add_fusion.1
  174.7 25.9 %online-softmax = f32[32,256,256]{2,1,0:T(8,128)} custom-call(f32[32,256,256]{2,1,0:T(8,128)} %copy-done, f32[32,256,256]{2,1,0:T(8,128)} %broadcast_add_fusion.1), custom_call_target="tpu_custom_call" | custom-call | tf_op online-softmax
  205.2 12.6 %fusion.114 = (f32[32,256]{1,0:T(8,128)S(1)}, f32[32,256]{1,0:T(8,128)S(1)}, f32[32,16,16,256]{3,0,2,1:T(8,128)}) fusion(f32[32,16,16,256]{3,0,2,1:T(8,128)} %get-tuple-element.252, f32[32,256,256]{2,1,0:T(8,128)S(1)} %broadcast_add_fusion), kind=kLoop, calls=%fused_computation.273 | loop fusion | flops 8372224 | bytes 25231360 | tf_op jit(solution)/shard_map/reduce_sum | solution.py:79
  223.7 22.8 %multiply_reduce_fusion.18 = (f32[32]{0:T(128)S(1)}, f32[32,16,16,3]{0,3,2,1:T(4,128)S(1)}) fusion(f32[32,16,16,3]{0,3,2,1:T(4,128)S(1)} %bitcast.356, bf16[32,16,16,256]{3,0,2,1:T(8,128)(2,1)S(1)} %multiply_convert_fusion.3, bf16[3,3,256,3]{2,3,1,0:T(4,128)(2,1)S(1)} %bitcast.366), kind=kOutput, calls=%fused_computation.144 | convolution fusion | flops 104079328 | bytes 4404864 | tf_op jit(solution)/shard_map/conv_general_dilated | solution.py:47
  247.2 8.6 multiply_reduce_fusion
  256.9 8.0 fusion.126
  271.9 6.9 fusion.44
  280.8 7.6 multiply_reduce_fusion.6
  288.5 6.4 convert_reduce_fusion
  313.5 6.8 fusion.88
  324.1 14.4 %multiply_reduce_fusion.12 = (f32[32,256]{1,0:T(8,128)S(1)}, f32[32,256]{1,0:T(8,128)S(1)}, f32[256]{0:T(256)S(1)}, f32[32,256,256]{2,1,0:T(8,128)}) fusion(f32[256]{0:T(256)S(1)} %bitcast.369, f32[32,256]{1,0:T(8,128)S(1)} %copy.287, f32[32,256]{1,0:T(8,128)S(1)} %copy.285, f32[32,256,256]{2,0,1:T(8,128)S(1)} %bitcast.329, ...), kind=kOutput, calls=%fused_computation.63 | convolution fusion | flops 1092599552 | bytes 38012928 | tf_op jit(solution)/shard_map/bpd,cd->bpc/dot_general | solution.py:307
  339.6 11.6 %copy.308 = f32[32,256,256]{2,0,1:T(8,128)} copy(f32[32,256,256]{2,1,0:T(8,128)} %get-tuple-element.259) | data formatting | bytes 16777216 | tf_op jit(solution)/shard_map/add | solution.py:305
  351.2 17.1 %multiply_reduce_fusion.1 = (f32[256]{0:T(256)S(1)}, f32[32,16,16,256]{3,0,2,1:T(8,128)}) fusion(f32[32,16,16,256]{3,0,2,1:T(8,128)} %bitcast.344, f32[32,16,16,256]{3,0,2,1:T(8,128)} %get-tuple-element.252, f32[32,256]{1,0:T(8,128)S(1)} %copy.287, f32[32,256]{1,0:T(8,128)S(1)} %copy.285, f32[32,16,16,256]{3,0,2,1:T(8,128)} %copy-done.1, ...), kind=kLoop, calls=%fused_computation.23 | loop fusion | flops 23068416 | bytes 42076160 | tf_op jit(solution)/shard_map/reduce_sum | solution.py:95
  368.3 14.5 %fusion.50 = f32[3,3,256,256]{3,2,1,0:T(8,128)} fusion(bf16[32,16,16,256]{3,0,2,1:T(8,128)(2,1)S(1)} %copy-done.20, f32[32,16,16,256]{3,0,2,1:T(8,128)} %get-tuple-element.211), kind=kOutput, calls=%fused_computation.101 | convolution fusion | flops 8877244416 | bytes 14942208 | tf_op jit(solution)/shard_map/conv_general_dilated | solution.py:53
  382.9 21.4 %multiply_reduce_fusion.2 = (f32[256]{0:T(256)S(1)}, f32[32,256]{1,0:T(8,128)S(1)}, f32[32,256]{1,0:T(8,128)S(1)}, f32[256]{0:T(256)S(1)}, f32[32,16,16,256]{3,0,2,1:T(8,128)}) fusion(f32[32,256]{1,0:T(8,128)S(1)} %copy-done.43, f32[32,256]{1,0:T(8,128)S(1)} %copy-done.41, f32[32,256]{1,0:T(8,128)S(1)} %copy-done.39, f32[32,16,16,256]{3,0,2,1:T(8,128)S(1)} %bitcast.342, ...), kind=kOutput, calls=%fused_computation.24 | convolution fusion | flops 8923365376 | bytes 34903040 | tf_op jit(solution)/shard_map/conv_general_dilated | solution.py:47
  405.5 7.8 fusion.113
  416.2 280.1 %fusion.47 = f32[3,3,256,256]{3,2,1,0:T(8,128)} fusion(bf16[32,16,16,256]{3,0,2,1:T(8,128)(2,1)S(1)} %copy-done.18, bf16[32,16,16,256]{3,0,2,1:T(8,128)(2,1)S(1)} %get-tuple-element.203), kind=kOutput, calls=%fused_computation.98 | convolution fusion | flops 8875147264 | bytes 10747904 | tf_op jit(solution)/shard_map/conv_general_dilated | solution.py:53
  696.8 16.8 %fusion.56 = f32[1,256,256]{2,1,0:T(8,128)S(1)} fusion(f32[32,256,256]{2,0,1:T(8,128)S(1)} %bitcast.326, f32[32,256,256]{2,0,1:T(8,128)} %bitcast.338, f32[32,256]{1,0:T(8,128)S(1)} %copy-done.45, f32[32,256]{1,0:T(8,128)S(1)} %copy-done.36, f32[32,256]{1,0:T(8,128)S(1)} %copy-done.34, f32[32,256]{1,0:T(8,128)S(1)} %copy-done.47, ...), kind=kOutput, calls=%fused_computation.115 | convolution fusion | flops 1092616192 | bytes 25559040 | tf_op jit(solution)/shard_map/bpc,bpd->cd/dot_general | solution.py:283
  720.9 20.6 %multiply_reduce_fusion.3 = (f32[256]{0:T(256)S(1)}, f32[32,256]{1,0:T(8,128)S(1)}, f32[32,256]{1,0:T(8,128)S(1)}, f32[256]{0:T(256)S(1)}, f32[32,16,16,256]{3,0,2,1:T(8,128)}) fusion(f32[32,256]{1,0:T(8,128)S(1)} %copy-done.48, f32[32,256]{1,0:T(8,128)S(1)} %copy-done.49, f32[32,16,16,256]{3,0,2,1:T(8,128)} %get-tuple-element.250, f32[256]{0:T(256)S(1)} %bitcast.377, ...), kind=kOutput, calls=%fused_computation.25 | convolution fusion | flops 8917073920 | bytes 22287360 | tf_op jit(solution)/shard_map/conv_general_dilated | solution.py:47
  742.7 10.6 %fusion.127 = (f32[256]{0:T(256)S(1)}, bf16[32,16,16,256]{3,0,2,1:T(8,128)(2,1)S(1)}, f32[256]{0:T(256)S(1)}) fusion(f32[32,16,16,256]{3,0,2,1:T(8,128)} %get-tuple-element.211, f32[32,256]{1,0:T(8,128)S(1)} %copy.325, f32[32,256]{1,0:T(8,128)S(1)} %copy-done.48, f32[32,256]{1,0:T(8,128)S(1)} %copy-done.49, f32[32,16,16,256]{3,0,2,1:T(8,128)} %get-tuple-element.250, ...), kind=kLoop, calls=%fused_computation.276 | loop fusion | flops 27262464 | bytes 29495296 | tf_op jit(solution)/shard_map/reduce_sum | solution.py:347
  755.3 7.1 fusion.104
  762.4 43.0 %all-reduce.6 = (f32[27,256]{1,0:T(8,128)S(1)}, f32[3,2304]{1,0:T(4,128)S(1)}, f32[19,256]{1,0:T(8,128)S(1)}, f32[]{:T(128)}) all-reduce(f32[27,256]{1,0:T(8,128)S(1)} %reshape.360, f32[3,2304]{1,0:T(4,128)S(1)} %bitcast.365, f32[19,256]{1,0:T(8,128)S(1)} %concatenate.12, ...), channel_id=1, replica_groups=mesh['batch'=8,'rows'=4] {'batch','rows'}, use_global_device_ids=true, to_apply=%region_36.37 | all-reduce | flops 18689 | bytes 149512 | tf_op jit(solution)/shard_map/psum | solution.py:361
  807.3 86.1 %all-reduce.5.cloned.1.call-done = (f32[2,2304,256]{2,1,0:T(8,128)}, f32[4,256,256]{2,1,0:T(8,128)}, f32[640,512]{1,0:T(8,128)}, f32[512,256]{1,0:T(8,128)}) async-done(((f32[2,2304,256]{2,1,0:T(8,128)}, f32[4,256,256]{2,1,0:T(8,128)}, f32[640,512]{1,0:T(8,128)}, f32[512,256]{1,0:T(8,128)}), (f32[2,2304,256]{2,1,0:T(8,128)}, f32[4,256,256]{2,1,0:T(8,128)}, f32[640,512]{1,0:T(8,128)}, ...) | async-done | bytes 7602192 | tf_op jit(solution)/shard_map/psum | solution.py:361
  928.8 12.0 %all-gather.5.cloned.1.call-done = f32[2,4,256,256]{3,2,1,0:T(8,128)} async-done(((f32[2,4,32,256]{3,2,1,0:T(8,128)}), f32[2,4,256,256]{3,2,1,0:T(8,128)}) %all-gather.5.cloned.1.call-update) | async-done | bytes 2097168 | tf_op jit(solution)/shard_map/all_gather | solution.py:423
  940.8 92.5 %all-gather.3.cloned.1.call-done = f32[2,2,2304,256]{3,2,1,0:T(8,128)} async-done(((f32[2,2,288,256]{3,2,1,0:T(8,128)}), f32[2,2,2304,256]{3,2,1,0:T(8,128)}) %all-gather.3.cloned.1.call-update) | async-done | bytes 9437200 | tf_op jit(solution)/shard_map/all_gather | solution.py:422
  1033.3 8.2 copy.459
  (416 shorter events, 185.5 us)
Async XLA Ops:
  9.7 20.0 %all-to-all-start = ((f32[4,1,6144]{2,1,0:T(1,128)}), f32[4,1,6144]{2,1,0:T(1,128)}, u32[]{:S(2)}, u32[]{:S(2)}) async-start(f32[4,1,6144]{2,1,0:T(1,128)} %reshape.376), calls=%async_computation | async-start | bytes 196608 | tf_op jit(solution)/shard_map/all_to_all | solution.py:207
  16.9 48.5 %copy-start.73 = (f32[1,256]{1,0:T(1,128)}, f32[1,256]{1,0:T(1,128)S(1)}, u32[]{:S(2)}) copy-start(f32[1,256]{1,0:T(1,128)S(1)} %get-tuple-element.234) | copy-start | bytes 3076
  29.7 25.2 %all-to-all-start.1 = ((f32[4,1,6144]{2,1,0:T(1,128)}), f32[4,1,6144]{2,1,0:T(1,128)S(1)}, u32[]{:S(2)}, u32[]{:S(2)}) async-start(f32[4,1,6144]{2,1,0:T(1,128)} %reshape.374), calls=%async_computation.1 | async-start | bytes 196608 | tf_op jit(solution)/shard_map/all_to_all | solution.py:208
  54.9 51.8 %all-to-all-start.2 = ((bf16[128,4,16,256]{3,2,1,0:T(8,128)(2,1)}), bf16[128,4,16,256]{3,2,1,0:T(8,128)(2,1)}, u32[]{:S(2)}, u32[]{:S(2)}) async-start(bf16[128,4,16,256]{3,2,1,0:T(8,128)(2,1)} %convert_element_type.138), calls=%async_computation.2 | async-start | bytes 8388608 | tf_op jit(solution)/shard_map/all_to_all | solution.py:209
  59.7 833.6 %all-reduce.5.cloned.1.call-start = ((), (), s32[]{:S(2)}) async-start(), calls=%async_computation.5 | async-start | bytes 15204352 | tf_op jit(solution)/shard_map/psum | solution.py:361
  95.5 28.2 %copy-start.40 = (f32[32,256]{1,0:T(8,128)}, f32[32,256]{1,0:T(8,128)S(1)}, u32[]{:S(2)}) copy-start(f32[32,256]{1,0:T(8,128)S(1)} %copy.280) | copy-start | bytes 98308
  95.6 28.1 %copy-start.42 = (f32[32,256]{1,0:T(8,128)}, f32[32,256]{1,0:T(8,128)S(1)}, u32[]{:S(2)}) copy-start(f32[32,256]{1,0:T(8,128)S(1)} %copy.282) | copy-start | bytes 98308
  174.7 25.9 %copy-start.83 = (f32[1,256]{1,0:T(1,128)S(1)}, f32[1,256]{1,0:T(1,128)}, u32[]{:S(2)}) copy-start(f32[1,256]{1,0:T(1,128)} %get-tuple-element.222) | copy-start | bytes 3076
  218.2 38.7 %copy-start.33 = (f32[32,256]{1,0:T(8,128)}, f32[32,256]{1,0:T(8,128)S(1)}, u32[]{:S(2)}) copy-start(f32[32,256]{1,0:T(8,128)S(1)} %copy.294) | copy-start | bytes 98308
  218.3 38.6 %copy-start.35 = (f32[32,256]{1,0:T(8,128)}, f32[32,256]{1,0:T(8,128)S(1)}, u32[]{:S(2)}) copy-start(f32[32,256]{1,0:T(8,128)S(1)} %copy.296) | copy-start | bytes 98308
  218.3 28.9 %slice-start.2 = ((s8[8388608]{0:T(1024)(128)(4,1)}), s8[4194304]{0:T(1024)(128)(4,1)S(1)}, s32[]{:S(2)}) async-start(s8[8388608]{0:T(1024)(128)(4,1)} %bitcast.322), calls=%async_computation.8 | async-start | bytes 8388608
  218.3 28.2 %copy-start.92 = (f32[32]{0:T(128)S(1)}, f32[32]{0:T(128)}, u32[]{:S(2)}) copy-start(f32[32]{0:T(128)} %copy-done.91) | copy-start | bytes 388
  218.4 28.8 %slice-start.3 = ((s8[8388608]{0:T(1024)(128)(4,1)}), s8[4194304]{0:T(1024)(128)(4,1)S(1)}, s32[]{:S(2)}) async-start(s8[8388608]{0:T(1024)(128)(4,1)} %bitcast.322), calls=%async_computation.9 | async-start | bytes 8388608
  218.4 28.8 %copy-start.70 = (bf16[9,3,256]{2,1,0:T(4,128)(2,1)S(1)}, bf16[9,3,256]{2,1,0:T(4,128)(2,1)}, u32[]{:S(2)}) copy-start(bf16[9,3,256]{2,1,0:T(4,128)(2,1)} %copy.298) | copy-start | bytes 41476
  223.7 32.1 %copy-start.16 = (bf16[32,16,16,256]{3,0,2,1:T(8,128)(2,1)}, bf16[32,16,16,256]{3,0,2,1:T(8,128)(2,1)S(1)}, u32[]{:S(2)}) copy-start(bf16[32,16,16,256]{3,0,2,1:T(8,128)(2,1)S(1)} %multiply_convert_fusion.3) | copy-start | bytes 12582916
  339.6 43.2 %slice-start.12 = ((s8[8388608]{0:T(1024)(128)(4,1)}), s8[4194304]{0:T(1024)(128)(4,1)S(1)}, s32[]{:S(2)}) async-start(s8[8388608]{0:T(1024)(128)(4,1)} %bitcast.341), calls=%async_computation.18 | async-start | bytes 8388608
  351.2 31.7 %slice-start.13 = ((s8[8388608]{0:T(1024)(128)(4,1)}), s8[4194304]{0:T(1024)(128)(4,1)S(1)}, s32[]{:S(2)}) async-start(s8[8388608]{0:T(1024)(128)(4,1)} %bitcast.341), calls=%async_computation.19 | async-start | bytes 8388608
  405.5 291.2 %slice-start.4 = ((s8[8388608]{0:T(1024)(128)(4,1)}), s8[4194304]{0:T(1024)(128)(4,1)S(1)}, s32[]{:S(2)}) async-start(s8[8388608]{0:T(1024)(128)(4,1)} %bitcast.324), calls=%async_computation.10 | async-start | bytes 8388608
  405.5 291.2 %slice-start.8 = ((s8[8388608]{0:T(1024)(128)(4,1)}), s8[4194304]{0:T(1024)(128)(4,1)S(1)}, s32[]{:S(2)}) async-start(s8[8388608]{0:T(1024)(128)(4,1)} %bitcast.330), calls=%async_computation.14 | async-start | bytes 8388608
  413.3 283.1 %copy-start.21 = (bf16[32,16,16,256]{3,0,2,1:T(8,128)(2,1)}, bf16[32,16,16,256]{3,0,2,1:T(8,128)(2,1)S(1)}, u32[]{:S(2)}) copy-start(bf16[32,16,16,256]{3,0,2,1:T(8,128)(2,1)S(1)} %get-tuple-element.203) | copy-start | bytes 12582916
  416.1 280.2 %copy-start.60 = (bf16[32,64]{1,0:T(8,128)(2,1)S(1)}, bf16[32,64]{1,0:T(8,128)(2,1)}, u32[]{:S(2)}) copy-start(bf16[32,64]{1,0:T(8,128)(2,1)} %copy-done.59) | copy-start | bytes 12292
  416.1 280.2 %copy-start.62 = (bf16[32,64]{1,0:T(8,128)(2,1)S(1)}, bf16[32,64]{1,0:T(8,128)(2,1)}, u32[]{:S(2)}) copy-start(bf16[32,64]{1,0:T(8,128)(2,1)} %copy-done.61) | copy-start | bytes 12292
  416.1 280.6 %slice-start.5 = ((s8[8388608]{0:T(1024)(128)(4,1)}), s8[4194304]{0:T(1024)(128)(4,1)S(1)}, s32[]{:S(2)}) async-start(s8[8388608]{0:T(1024)(128)(4,1)} %bitcast.324), calls=%async_computation.11 | async-start | bytes 8388608
  416.1 280.6 %slice-start.9 = ((s8[8388608]{0:T(1024)(128)(4,1)}), s8[4194304]{0:T(1024)(128)(4,1)S(1)}, s32[]{:S(2)}) async-start(s8[8388608]{0:T(1024)(128)(4,1)} %bitcast.330), calls=%async_computation.15 | async-start | bytes 8388608
  416.1 280.6 %copy-start.34 = (f32[32,256]{1,0:T(8,128)S(1)}, f32[32,256]{1,0:T(8,128)}, u32[]{:S(2)}) copy-start(f32[32,256]{1,0:T(8,128)} %copy-done.33) | copy-start | bytes 98308
  416.2 280.6 %copy-start.36 = (f32[32,256]{1,0:T(8,128)S(1)}, f32[32,256]{1,0:T(8,128)}, u32[]{:S(2)}) copy-start(f32[32,256]{1,0:T(8,128)} %copy-done.35) | copy-start | bytes 98308
  416.2 280.6 %copy-start.45 = (f32[32,256]{1,0:T(8,128)S(1)}, f32[32,256]{1,0:T(8,128)}, u32[]{:S(2)}) copy-start(f32[32,256]{1,0:T(8,128)} %copy-done.44) | copy-start | bytes 98308
  416.2 280.6 %copy-start.47 = (f32[32,256]{1,0:T(8,128)S(1)}, f32[32,256]{1,0:T(8,128)}, u32[]{:S(2)}) copy-start(f32[32,256]{1,0:T(8,128)} %copy-done.46) | copy-start | bytes 98308
  720.8 220.0 %all-gather.5.cloned.1.call-start = ((), (), s32[]{:S(2)}) async-start(), calls=%async_computation.4 | async-start | bytes 2359296 | tf_op jit(solution)/shard_map/all_gather | solution.py:423
  755.3 153.0 %copy-start.52 = (f32[2,4,32,256]{3,2,1,0:T(8,128)S(1)}, f32[2,4,32,256]{3,2,1,0:T(8,128)}, u32[]{:S(2)}) copy-start(f32[2,4,32,256]{3,2,1,0:T(8,128)} %param.41) | copy-start | bytes 786436
  755.3 153.0 %copy-start.57 = (f32[4,32,256]{2,1,0:T(8,128)S(1)}, f32[4,32,256]{2,1,0:T(8,128)}, u32[]{:S(2)}) copy-start(f32[4,32,256]{2,1,0:T(8,128)} %param.48) | copy-start | bytes 393220
  910.9 122.5 %all-gather.3.cloned.1.call-start = ((), (), s32[]{:S(2)}) async-start(), calls=%async_computation.3 | async-start | bytes 10616832 | tf_op jit(solution)/shard_map/all_gather | solution.py:422
  (90 other events, 912.4 us)
Sparse Core Ops, SparseCore 0:
  720.9 172.3 all-reduce.4
  911.0 29.7 all-gather.4
  943.0 90.2 all-gather.2
